TPU v7x, 256 devices: a whole 4x4x8 slice. The times are simulated.
256 devices in a mesh: grp: 16 (over y_hi, x, core), dev: 16 (over z, y_lo).
Axes of the slice: x: 4, y: 4 (y_hi: 2, y_lo: 2; y = y_hi * 2 + y_lo), z: 8, core: 2. Of those that a mesh axis runs over, the one named last changes fastest.
Arguments:
- start: float32 [67108864], P(('grp', 'dev')), may hold values from -18 to 18
- hopping: float32 [5, 256, 256], replicated, may hold values from -0.2 to 1.2
- blocks: float32 [5, 256, 256], replicated, may hold values from -0.2 to 1.2
Outputs:
- basis_next: float32 [2, 67108864], P(None, ('grp', 'dev'))
- hessenberg: float32 [5], replicated
All inputs are finite; a program needn't handle non-finite values.
Results may differ from a plain program's by a relative error of at most 0.00013.
Values sent between devices are 32-bit elements; how exact they have to be, the bound alone decides.
A program may use at most 64 MiB of HBM per device.

v0:
```python
import functools

import jax
import jax.numpy as jnp
from jax import lax
from jax.sharding import Mesh
from jax.sharding import PartitionSpec as P

GRP = ("grp_0", "grp_1", "grp_2")
DEV = ("dev_0", "dev_1")
GRP_DEV = ("grp_0", "grp_1", "grp_2", "dev_0", "dev_1")


def in_blocks(value, dim, count):
    shape = value.shape
    tiles = value.reshape(*shape[:dim], count, shape[dim] // count, *shape[dim + 1 :])
    return jnp.moveaxis(tiles, dim, 0)


def joined_along(tiles, dim):
    tiles = jnp.moveaxis(tiles, 0, dim)
    shape = tiles.shape
    return tiles.reshape(*shape[:dim], shape[dim] * shape[dim + 1], *shape[dim + 2 :])


def one_exchange(value, axis, axes, splits, concats):
    sizes = [lax.axis_size(a) for a in axes]
    tiles = in_blocks(value, splits[0], sizes[0])
    tiles = jnp.moveaxis(in_blocks(tiles, splits[1] + 1, sizes[1]), 0, 1)
    inside = tiles.shape[2:]
    tiles = tiles.reshape(-1, *inside)
    tiles = lax.all_to_all(tiles, axis, split_axis=0, concat_axis=0, tiled=True)
    tiles = joined_along(tiles.reshape(*sizes, *inside), concats[0] + 1)
    return joined_along(tiles, concats[1])


def over_axes(value, axes):
    return functools.reduce(lax.psum, axes, value)


def window_apply(vector, matrix, first):
    order = matrix.shape[0]
    if first == 0:
        block = vector.reshape(-1, order)
        return jnp.einsum("pk,bk->bp", matrix, block, precision=lax.Precision.HIGHEST).reshape(-1)
    block = vector.reshape(-1, order, 2**first)
    return jnp.einsum("pk,bkl->bpl", matrix, block, precision=lax.Precision.HIGHEST).reshape(-1)


def per_device(start, hopping, blocks):
    n_grp = lax.axis_size(GRP)
    n_dev = lax.axis_size(DEV)
    gbits = (n_grp * n_dev).bit_length() - 1
    count = start.shape[0]
    sites = count.bit_length() - 1 + gbits
    window = hopping.shape[1].bit_length() - 1
    states = float(2**sites)
    lowbits = sites - 11 - gbits
    middle = 2 ** (11 - gbits)
    starts = (
        0,
        min(window - 1, sites - 8 - window),
        sites - 8 - window,
        sites - 11,
        sites - window,
    )

    def enter(field):
        return field.reshape(1, 1, middle, n_grp, n_dev, 2**lowbits)

    def leave(field):
        return field.reshape(n_grp, n_dev, middle, 1, 1, 2**lowbits)

    def native(field, matrix, index):
        return window_apply(field, matrix, starts[index])

    def swapped(field, matrix, index):
        return window_apply(field, matrix, starts[index] - gbits)

    def lower_terms(vector):
        total = native(vector, hopping[0], 0)
        total = total + native(vector, hopping[1], 1)
        return total + native(vector, hopping[2], 2)

    def precond_image(vector):
        partial_sum = lower_terms(vector)
        moved_vec, moved_part = (
            one_exchange(enter(vector), GRP_DEV, (GRP, DEV), (3, 4), (0, 1)),
            one_exchange(enter(partial_sum), GRP_DEV, (GRP, DEV), (3, 4), (0, 1)),
        )
        moved_vec = moved_vec.reshape(-1)
        total = (
            moved_part.reshape(-1)
            + swapped(moved_vec, hopping[3], 3)
            + swapped(moved_vec, hopping[4], 4)
        )
        total = swapped(total, blocks[4], 4)
        total = swapped(total, blocks[3], 3)
        total = one_exchange(leave(total), GRP_DEV, (GRP, DEV), (0, 1), (3, 4)).reshape(-1)
        for index in (2, 1, 0):
            total = native(total, blocks[index], index)
        return total

    def arnoldi(basis, vector):
        image = precond_image(vector)
        local = jnp.stack([jnp.sum(b * image) for b in basis])
        sums = (over_axes(local, GRP_DEV), over_axes(jnp.sum(image * image), GRP_DEV))
        coeffs = sums[0] / states
        square = sums[1] / states - jnp.sum(coeffs * coeffs)
        for index in range(len(basis)):
            image = image - coeffs[index] * basis[index]
        length = jnp.sqrt(square + 1e-06)
        return (image / length, coeffs, length)

    start_square = over_axes(jnp.sum(start * start), GRP_DEV) / states
    first = start / jnp.sqrt(start_square + 1e-06)
    second, coeffs_one, length_one = arnoldi([first], first)
    third, coeffs_two, length_two = arnoldi([first, second], second)
    basis_next = jnp.stack([second, third])
    hessenberg = jnp.stack([coeffs_one[0], length_one, coeffs_two[0], coeffs_two[1], length_two])
    return (basis_next, hessenberg)


def solution(mesh):
    finer = Mesh(mesh.devices.reshape(2, 4, 2, 8, 2), ("grp_0", "grp_1", "grp_2", "dev_0", "dev_1"))
    placed = (P(GRP_DEV), P(), P())
    return jax.shard_map(
        per_device, mesh=finer, in_specs=placed, out_specs=(P(None, GRP_DEV), P()), check_vma=False
    )
```

profile of v0, /device:TPU:32, one launch (start us, length us, event | category | flops | bytes accessed | tf_op | source)
XLA Modules:
  0.0 515.4 jit_solution(472283645054011477)
XLA Ops:
  2.8 7.0 %psum.175 = f32[]{:T(128)} all-reduce(f32[]{:T(128)} %multiply_reduce_fusion.5), channel_id=1, replica_groups=mesh['grp_0'=2,'grp_1'=4,'grp_2'=2,'dev_0'=8,'dev_1'=2] {'grp_0'}, use_global_device_ids=true, to_apply=%region_1.0 | all-reduce | flops 1 | bytes 8 | tf_op jit(solution)/shard_map/psum | solution.py:38
  9.9 11.1 %psum.176 = f32[]{:T(128)} all-reduce(f32[]{:T(128)} %psum.175), channel_id=1, replica_groups=mesh['grp_0'=2,'grp_1'=4,'grp_2'=2,'dev_0'=8,'dev_1'=2] {'grp_1'}, use_global_device_ids=true, to_apply=%region_2.0 | all-reduce | flops 1 | bytes 8 | tf_op jit(solution)/shard_map/psum | solution.py:38
  21.0 3.1 psum.177
  24.0 18.5 %psum.178 = f32[]{:T(128)} all-reduce(f32[]{:T(128)} %psum.177), channel_id=1, replica_groups=mesh['grp_0'=2,'grp_1'=4,'grp_2'=2,'dev_0'=8,'dev_1'=2] {'dev_0'}, use_global_device_ids=true, to_apply=%region_4.0 | all-reduce | flops 1 | bytes 8 | tf_op jit(solution)/shard_map/psum | solution.py:38
  42.5 5.5 %psum.179 = f32[]{:T(128)} all-reduce(f32[]{:T(128)} %psum.178), channel_id=1, replica_groups=mesh['grp_0'=2,'grp_1'=4,'grp_2'=2,'dev_0'=8,'dev_1'=2] {'dev_1'}, use_global_device_ids=true, to_apply=%region_5.0 | all-reduce | flops 1 | bytes 8 | tf_op jit(solution)/shard_map/psum | solution.py:38
  51.5 4.0 convolution_bitcast_fusion.14
  55.6 2.5 copy.73
  58.1 2.4 reshape.244
  60.5 3.2 fusion.30
  66.0 2.8 convolution_bitcast_fusion.15
  68.8 2.5 copy.72
  75.0 10.5 %all-to-all-start = ((f32[256,1,1,8,1,1,128]{6,3,5,4,2,1,0:T(8,128)}), f32[256,1,1,8,1,1,128]{6,3,5,4,2,1,0:T(8,128)}, u32[]{:S(2)}, u32[]{:S(2)}) async-start(f32[256,1,1,8,1,1,128]{6,3,5,4,2,1,0:T(8,128)} %copy.74), calls=%async_computation | async-start | bytes 2097152 | tf_op jit(solution)/shard_map/all_to_all | solution.py:32
  87.1 27.0 %all-to-all-done = f32[256,1,1,8,1,1,128]{6,3,5,4,2,1,0:T(8,128)} async-done(((f32[256,1,1,8,1,1,128]{6,3,5,4,2,1,0:T(8,128)}), f32[256,1,1,8,1,1,128]{6,3,5,4,2,1,0:T(8,128)}, u32[]{:S(2)}, u32[]{:S(2)}) %all-to-all-start) | async-done | bytes 1048608 | tf_op jit(solution)/shard_map/all_to_all | solution.py:32
  114.1 7.8 %all-to-all-start.1 = ((f32[256,1,1,8,1,1,128]{6,3,5,4,2,1,0:T(8,128)}), f32[256,1,1,8,1,1,128]{6,3,5,4,2,1,0:T(8,128)S(1)}, u32[]{:S(2)}, u32[]{:S(2)}) async-start(f32[256,1,1,8,1,1,128]{6,3,5,4,2,1,0:T(8,128)} %copy.75), calls=%async_computation.1 | async-start | bytes 2097152 | tf_op jit(solution)/shard_map/all_to_all | solution.py:32
  121.9 3.6 copy.78
  125.5 25.7 %all-to-all-done.1 = f32[256,1,1,8,1,1,128]{6,3,5,4,2,1,0:T(8,128)S(1)} async-done(((f32[256,1,1,8,1,1,128]{6,3,5,4,2,1,0:T(8,128)}), f32[256,1,1,8,1,1,128]{6,3,5,4,2,1,0:T(8,128)S(1)}, u32[]{:S(2)}, u32[]{:S(2)}) %all-to-all-start.1) | async-done | bytes 1048608 | tf_op jit(solution)/shard_map/all_to_all | solution.py:32
  151.3 2.8 convolution_bitcast_fusion.13
  154.0 2.6 copy.77
  156.6 2.4 reshape.253
  159.0 2.6 copy.79
  161.6 3.4 fusion.1
  168.9 3.0 convolution_bitcast_fusion.10
  173.3 37.4 %all_to_all.30 = f32[256,1,1,8,1,1,128]{6,3,5,4,2,1,0:T(8,128)S(1)} all-to-all(f32[256,1,1,8,1,1,128]{6,3,5,4,2,1,0:T(8,128)} %bitcast.281), channel_id=1, replica_groups=mesh['grp_0'=2,'grp_1'=4,'grp_2'=2,'dev_0'=8,'dev_1'=2] {'grp_0','grp_1'..., dimensions={0} | all-to-all | bytes 2097152 | tf_op jit(solution)/shard_map/all_to_all | solution.py:32
  212.0 3.0 convolution_bitcast_fusion.9
  217.7 2.8 convolution_bitcast_fusion.8
  220.5 2.5 copy.87
  227.6 7.0 %all-reduce.9 = (f32[]{:T(128)}, f32[1]{0:T(128)}) all-reduce(f32[]{:T(128)} %get-tuple-element.28, f32[1]{0:T(128)} %bitcast.57), channel_id=1, replica_groups=mesh['grp_0'=2,'grp_1'=4,'grp_2'=2,'dev_0'=8,'dev_1'=2] {'grp_0'}, use_global_device_ids=true, to_apply=%region_13.0 | all-reduce | flops 2 | bytes 16 | tf_op jit(solution)/shard_map/psum | solution.py:38
  234.7 11.1 %all-reduce.3 = (f32[]{:T(128)}, f32[1]{0:T(128)}) all-reduce(f32[]{:T(128)} %get-tuple-element.22, f32[1]{0:T(128)} %get-tuple-element.23), channel_id=1, replica_groups=mesh['grp_0'=2,'grp_1'=4,'grp_2'=2,'dev_0'=8,'dev_1'=2] {'grp_1'}, use_global_device_ids=true, to_apply=%region_14.0 | all-reduce | flops 2 | bytes 16 | tf_op jit(solution)/shard_map/psum | solution.py:38
  245.8 3.1 all-reduce.7
  248.8 15.7 %all-reduce.1 = (f32[]{:T(128)}, f32[1]{0:T(128)}) all-reduce(f32[]{:T(128)} %get-tuple-element.18, f32[1]{0:T(128)} %get-tuple-element.19), channel_id=1, replica_groups=mesh['grp_0'=2,'grp_1'=4,'grp_2'=2,'dev_0'=8,'dev_1'=2] {'dev_0'}, use_global_device_ids=true, to_apply=%region_16.0 | all-reduce | flops 2 | bytes 16 | tf_op jit(solution)/shard_map/psum | solution.py:38
  264.6 5.7 %all-reduce.5 = (f32[]{:T(128)}, f32[1]{0:T(128)}) all-reduce(f32[]{:T(128)} %get-tuple-element.6, f32[1]{0:T(128)} %get-tuple-element.7), channel_id=1, replica_groups=mesh['grp_0'=2,'grp_1'=4,'grp_2'=2,'dev_0'=8,'dev_1'=2] {'dev_1'}, use_global_device_ids=true, to_apply=%region_17.0 | all-reduce | flops 2 | bytes 16 | tf_op jit(solution)/shard_map/psum | solution.py:38
  275.8 4.0 convolution_bitcast_fusion.6
  279.8 2.5 copy.90
  282.3 2.4 reshape.265
  284.7 3.2 fusion.28
  290.2 2.8 convolution_bitcast_fusion.7
  293.0 2.6 copy.89
  299.0 6.7 %all-to-all-start.3 = ((f32[256,1,1,8,1,1,128]{6,3,5,4,2,1,0:T(8,128)}), f32[256,1,1,8,1,1,128]{6,3,5,4,2,1,0:T(8,128)S(1)}, u32[]{:S(2)}, u32[]{:S(2)}) async-start(f32[256,1,1,8,1,1,128]{6,3,5,4,2,1,0:T(8,128)} %copy.91), calls=%async_computation.3 | async-start | bytes 2097152 | tf_op jit(solution)/shard_map/all_to_all | solution.py:32
  307.3 27.9 %all-to-all-done.3 = f32[256,1,1,8,1,1,128]{6,3,5,4,2,1,0:T(8,128)S(1)} async-done(((f32[256,1,1,8,1,1,128]{6,3,5,4,2,1,0:T(8,128)}), f32[256,1,1,8,1,1,128]{6,3,5,4,2,1,0:T(8,128)S(1)}, u32[]{:S(2)}, u32[]{:S(2)}) %all-to-all-start.3) | async-done | bytes 1048608 | tf_op jit(solution)/shard_map/all_to_all | solution.py:32
  336.2 7.8 %all-to-all-start.4 = ((f32[256,1,1,8,1,1,128]{6,3,5,4,2,1,0:T(8,128)}), f32[256,1,1,8,1,1,128]{6,3,5,4,2,1,0:T(8,128)S(1)}, u32[]{:S(2)}, u32[]{:S(2)}) async-start(f32[256,1,1,8,1,1,128]{6,3,5,4,2,1,0:T(8,128)} %copy.92), calls=%async_computation.4 | async-start | bytes 2097152 | tf_op jit(solution)/shard_map/all_to_all | solution.py:32
  344.0 3.6 copy.95
  347.6 25.7 %all-to-all-done.4 = f32[256,1,1,8,1,1,128]{6,3,5,4,2,1,0:T(8,128)S(1)} async-done(((f32[256,1,1,8,1,1,128]{6,3,5,4,2,1,0:T(8,128)}), f32[256,1,1,8,1,1,128]{6,3,5,4,2,1,0:T(8,128)S(1)}, u32[]{:S(2)}, u32[]{:S(2)}) %all-to-all-start.4) | async-done | bytes 1048608 | tf_op jit(solution)/shard_map/all_to_all | solution.py:32
  373.4 3.7 convolution_bitcast_fusion.5
  377.1 2.6 copy.94
  379.7 2.4 reshape.274
  382.1 2.6 copy.96
  384.7 3.4 fusion.3
  391.4 2.5 reshape_reshape.39
  393.9 4.0 convolution_bitcast_fusion.2
  397.9 2.5 copy.99
  400.4 37.2 %all_to_all.31 = f32[256,1,1,8,1,1,128]{6,3,5,4,2,1,0:T(8,128)S(1)} all-to-all(f32[256,1,1,8,1,1,128]{6,3,5,4,2,1,0:T(8,128)} %bitcast.284), channel_id=1, replica_groups=mesh['grp_0'=2,'grp_1'=4,'grp_2'=2,'dev_0'=8,'dev_1'=2] {'grp_0','grp_1'..., dimensions={0} | all-to-all | bytes 2097152 | tf_op jit(solution)/shard_map/all_to_all | solution.py:32
  438.8 2.4 reshape.279
  441.2 4.0 convolution_bitcast_fusion.1
  445.2 2.5 copy.102
  450.1 4.0 convolution_bitcast_fusion
  454.1 2.5 copy.104
  456.6 2.5 reshape_reshape.41
  459.1 2.9 multiply_reduce_fusion
  465.0 7.0 %all-reduce.8 = (f32[]{:T(128)}, f32[2]{0:T(128)S(1)}) all-reduce(f32[]{:T(128)} %get-tuple-element.30, f32[2]{0:T(128)S(1)} %pad_maximum_fusion.1), channel_id=1, replica_groups=mesh['grp_0'=2,'grp_1'=4,'grp_2'=2,'dev_0'=8,'dev_1'=2] {'grp_0'}, use_global_device_ids=true, to_apply=%region_26.0 | all-reduce | flops 3 | bytes 24 | tf_op jit(solution)/shard_map/psum | solution.py:38
  472.0 11.0 %all-reduce.2 = (f32[]{:T(128)}, f32[2]{0:T(128)S(1)}) all-reduce(f32[]{:T(128)} %get-tuple-element.20, f32[2]{0:T(128)S(1)} %get-tuple-element.21), channel_id=1, replica_groups=mesh['grp_0'=2,'grp_1'=4,'grp_2'=2,'dev_0'=8,'dev_1'=2] {'grp_1'}, use_global_device_ids=true, to_apply=%region_27.0 | all-reduce | flops 3 | bytes 24 | tf_op jit(solution)/shard_map/psum | solution.py:38
  483.1 3.1 all-reduce.6
  486.1 15.7 %all-reduce = (f32[]{:T(128)}, f32[2]{0:T(128)S(1)}) all-reduce(f32[]{:T(128)} %get-tuple-element.16, f32[2]{0:T(128)S(1)} %get-tuple-element.17), channel_id=1, replica_groups=mesh['grp_0'=2,'grp_1'=4,'grp_2'=2,'dev_0'=8,'dev_1'=2] {'dev_0'}, use_global_device_ids=true, to_apply=%region_29.0 | all-reduce | flops 3 | bytes 24 | tf_op jit(solution)/shard_map/psum | solution.py:38
  501.9 5.5 %all-reduce.4 = (f32[]{:T(128)}, f32[2]{0:T(128)S(1)}) all-reduce(f32[]{:T(128)} %get-tuple-element.4, f32[2]{0:T(128)S(1)} %get-tuple-element.5), channel_id=1, replica_groups=mesh['grp_0'=2,'grp_1'=4,'grp_2'=2,'dev_0'=8,'dev_1'=2] {'dev_1'}, use_global_device_ids=true, to_apply=%region_30.0 | all-reduce | flops 3 | bytes 24 | tf_op jit(solution)/shard_map/psum | solution.py:38
  512.0 2.9 pad_maximum_fusion
  (52 shorter events, 50.5 us)
Async XLA Ops:
  0.6 48.2 %copy-start = (f32[262144]{0:T(1024)S(1)}, f32[262144]{0:T(1024)}, u32[]{:S(2)}) copy-start(f32[262144]{0:T(1024)} %param.3) | copy-start | bytes 3145732
  50.0 1.5 copy-start.1
  75.0 39.1 %all-to-all-start = ((f32[256,1,1,8,1,1,128]{6,3,5,4,2,1,0:T(8,128)}), f32[256,1,1,8,1,1,128]{6,3,5,4,2,1,0:T(8,128)}, u32[]{:S(2)}, u32[]{:S(2)}) async-start(f32[256,1,1,8,1,1,128]{6,3,5,4,2,1,0:T(8,128)} %copy.74), calls=%async_computation | async-start | bytes 2097152 | tf_op jit(solution)/shard_map/all_to_all | solution.py:32
  114.1 37.2 %all-to-all-start.1 = ((f32[256,1,1,8,1,1,128]{6,3,5,4,2,1,0:T(8,128)}), f32[256,1,1,8,1,1,128]{6,3,5,4,2,1,0:T(8,128)S(1)}, u32[]{:S(2)}, u32[]{:S(2)}) async-start(f32[256,1,1,8,1,1,128]{6,3,5,4,2,1,0:T(8,128)} %copy.75), calls=%async_computation.1 | async-start | bytes 2097152 | tf_op jit(solution)/shard_map/all_to_all | solution.py:32
  167.3 1.7 copy-start.3
  274.2 1.5 copy-start.2
  293.0 2.6 copy-start.6
  299.0 36.2 %all-to-all-start.3 = ((f32[256,1,1,8,1,1,128]{6,3,5,4,2,1,0:T(8,128)}), f32[256,1,1,8,1,1,128]{6,3,5,4,2,1,0:T(8,128)S(1)}, u32[]{:S(2)}, u32[]{:S(2)}) async-start(f32[256,1,1,8,1,1,128]{6,3,5,4,2,1,0:T(8,128)} %copy.91), calls=%async_computation.3 | async-start | bytes 2097152 | tf_op jit(solution)/shard_map/all_to_all | solution.py:32
  335.2 1.0 copy-start.5
  336.2 37.2 %all-to-all-start.4 = ((f32[256,1,1,8,1,1,128]{6,3,5,4,2,1,0:T(8,128)}), f32[256,1,1,8,1,1,128]{6,3,5,4,2,1,0:T(8,128)S(1)}, u32[]{:S(2)}, u32[]{:S(2)}) async-start(f32[256,1,1,8,1,1,128]{6,3,5,4,2,1,0:T(8,128)} %copy.92), calls=%async_computation.4 | async-start | bytes 2097152 | tf_op jit(solution)/shard_map/all_to_all | solution.py:32
  391.4 2.5 copy-start.4
where the time goes:
time: 526 us; the launch traced here: 515 us
  blocking collectives  205 us (39%)
  waiting for transfers between devices  106 us (20%)
  local copies, waits for them, and re-layouts  87.5 us (17%)
  matrix products  62.6 us (12%)
  starting transfers between devices  32.9 us (6%)
  other arithmetic  15.1 us (3%)
  between operations  5.94 us (1%)
    psum x15, blocking collectives, over_axes(): return functools.reduce(lax.psum, axes, value)  130 us
    all_to_all x4, waiting for transfers between devices, one_exchange(): tiles = lax.all_to_all(tiles, axis, split_axis=0, concat_axis=0, tiled=True)  106 us
    all_to_all x2, blocking collectives, one_exchange(): tiles = lax.all_to_all(tiles, axis, split_axis=0, concat_axis=0, tiled=True)  74.6 us
    dot_general x16, matrix products, window_apply(): jnp.einsum('pk,bkl->bpl', matrix, block, precision=lax.Precision.HIGHEST)  51.7 us
    all_to_all x4, starting transfers between devices, one_exchange(): tiles = lax.all_to_all(tiles, axis, split_axis=0, concat_axis=0, tiled=True)  32.9 us
    transpose x14, local copies, waits for them, and re-layouts, window_apply(): jnp.einsum('pk,bkl->bpl', matrix, block, precision=lax.Precision.HIGHEST)  29.9 us
    reshape x6, local copies, waits for them, and re-layouts, window_apply(): jnp.einsum('pk,bkl->bpl', matrix, block, precision=lax.Precision.HIGHEST)  14.6 us
    dot_general x4, matrix products, window_apply(): jnp.einsum('pk,bk->bp', matrix, block, precision=lax.Precision.HIGHEST)  10.9 us
  transfers between devices with their start and end apart: 4, of which 4 were waited for; matrix products, arithmetic and copies ran while one was open for 2% of the time, Pallas kernels for 0%

commit v1 on v0

v1 whole, which is shorter than its diff:
```python
import functools

import jax
import jax.numpy as jnp
from jax import lax
from jax.experimental import pallas as pl
from jax.experimental.pallas import tpu as pltpu
from jax.sharding import PartitionSpec as P

MESH = pl.DeviceIdType.MESH
HI = lax.Precision.HIGHEST
AXES = ("grp", "dev")


def exchange_kernel(ng, nd, x_ref, o_ref, send_sem, recv_sem):
    n = ng * nd
    me = lax.axis_index("grp") * nd + lax.axis_index("dev")
    barrier = pltpu.get_barrier_semaphore()

    def greet(off, carry):
        to = lax.rem(me + off, n)
        pl.semaphore_signal(barrier, inc=1, device_id=(to // nd, to % nd), device_id_type=MESH)
        return carry

    lax.fori_loop(1, n, greet, 0)
    pl.semaphore_wait(barrier, n - 1)

    def send(off, carry):
        to = lax.rem(me + off, n)
        pltpu.make_async_remote_copy(
            src_ref=x_ref.at[to],
            dst_ref=o_ref.at[me],
            send_sem=send_sem,
            recv_sem=recv_sem,
            device_id=(to // nd, to % nd),
            device_id_type=MESH,
        ).start()
        return carry

    lax.fori_loop(1, n, send, 0)
    o_ref[me] = x_ref[me]
    pltpu.make_async_copy(x_ref.at[pl.ds(0, n - 1)], x_ref.at[pl.ds(0, n - 1)], send_sem).wait()
    pltpu.make_async_copy(o_ref.at[pl.ds(0, n - 1)], o_ref.at[pl.ds(0, n - 1)], recv_sem).wait()


def exchange(x, ng, nd):
    vmem = pl.BlockSpec(memory_space=pltpu.VMEM)
    return pl.pallas_call(
        functools.partial(exchange_kernel, ng, nd),
        out_shape=jax.ShapeDtypeStruct(x.shape, x.dtype),
        in_specs=[vmem],
        out_specs=vmem,
        scratch_shapes=[pltpu.SemaphoreType.DMA, pltpu.SemaphoreType.DMA],
        name="exchange",
        compiler_params=pltpu.CompilerParams(collective_id=0, has_side_effects=True),
    )(x)


def per_device(start, hopping, blocks):
    ng, nd = lax.axis_size("grp"), lax.axis_size("dev")
    tiles = ng * nd
    states = float(start.shape[0] * tiles)

    def local(which, mat, v):
        if which == 0:
            u = v.reshape(tiles // 2, 2, 8, 128)
            m = mat.reshape(2, 128, 2, 128)
            return jnp.einsum("apbk,tbsk->tasp", m, u, precision=HI).reshape(v.shape)
        if which in (1, 4):
            return jnp.einsum("pt,tsl->psl", mat, v, precision=HI)
        if which == 2:
            u = v.reshape(32, 8, 8, 128)
            m = mat.reshape(8, 32, 8, 32)
            return jnp.einsum("aphq,qbhl->pbal", m, u, precision=HI).reshape(v.shape)
        u = v.reshape(8, 256, 128)
        return jnp.einsum("pk,bkl->bpl", mat, u, precision=HI).reshape(v.shape)

    def apply(v):
        part = local(0, hopping[0], v) + local(1, hopping[1], v) + local(2, hopping[2], v)
        moved = exchange(v, ng, nd)
        total = exchange(part, ng, nd) + local(3, hopping[3], moved) + local(4, hopping[4], moved)
        total = local(3, blocks[3], local(4, blocks[4], total))
        total = exchange(total, ng, nd)
        for index in (2, 1, 0):
            total = local(index, blocks[index], total)
        return total

    def means(*values):
        return lax.psum(jnp.stack([jnp.sum(v) for v in values]), AXES) / states

    x = start.reshape(8, tiles, 128).transpose(1, 0, 2)
    first = x / jnp.sqrt(means(x * x)[0] + 1e-06)
    image = apply(first)
    h00, square = means(first * image, image * image)
    image = image - h00 * first
    r1 = jnp.sqrt(square - h00 * h00 + 1e-06)
    second = image / r1
    image = apply(second)
    h01, h11, square = means(first * image, second * image, image * image)
    r2 = jnp.sqrt(square - h01 * h01 - h11 * h11 + 1e-06)
    third = (image - h01 * first - h11 * second) / r2
    basis = jnp.stack([second, third]).transpose(0, 2, 1, 3).reshape(2, -1)
    return basis, jnp.stack([h00, r1, h01, h11, r2])


def solution(mesh):
    return jax.shard_map(
        per_device,
        mesh=mesh,
        in_specs=(P(AXES), P(), P()),
        out_specs=(P(None, AXES), P()),
        check_vma=False,
    )
```

time: 526 us -> 603 us (1.15)
  Pallas kernels: 0 us -> 228 us
  waiting for transfers between devices: 106 us -> 0 us
  local copies, waits for them, and re-layouts: 87.5 us -> 47.4 us
  starting transfers between devices: 32.9 us -> 0 us
  blocking collectives: 205 us -> 233 us
  matrix products: 62.6 us -> 55.4 us
  other arithmetic: 15.1 us -> 21.9 us
    pallas_call x0 -> x6, Pallas kernels: none -> 228 us  [exchange(): pl.pallas_call(functools.partial(exchange_kernel, ng, nd), out_shape=jax....]
    all_to_all x4 -> x0, waiting for transfers between devices: 106 us -> none  [one_exchange(): tiles = lax.all_to_all(tiles, axis, split_axis=0, concat_axis=0, tiled=True)]
    psum x15 -> x3, blocking collectives: 130 us -> 233 us  [means(): return lax.psum(jnp.stack([jnp.sum(v) for v in values]), AXES) / states]
    all_to_all x2 -> x0, blocking collectives: 74.6 us -> none  [one_exchange(): tiles = lax.all_to_all(tiles, axis, split_axis=0, concat_axis=0, tiled=True)]
    all_to_all x4 -> x0, starting transfers between devices: 32.9 us -> none  [one_exchange(): tiles = lax.all_to_all(tiles, axis, split_axis=0, concat_axis=0, tiled=True)]
    reshape x17 -> x0, local copies, waits for them, and re-layouts: 30.8 us -> none  [the longest x6 14.6 us: window_apply(): jnp.einsum('pk,bkl->bpl', matrix, block, precision=lax.Precision.HIGHEST)]
    another operation x11 -> x8, local copies, waits for them, and re-layouts: 23.2 us -> 7.68 us  [the longest x4 4.53 us: local(): m = mat.reshape(8, 32, 8, 32)]
    transpose x14 -> x13, local copies, waits for them, and re-layouts: 29.9 us -> 15 us  [the longest x4 6.68 us: local(): return jnp.einsum('pk,bkl->bpl', mat, u, precision=HI).reshape(v.shape)]
  transfers between devices with their start and end apart: 4 -> 0, of which waited for: 4 -> 0; matrix products, arithmetic and copies ran while one was open for 2% -> 0% of each run, Pallas kernels for 0% -> 0%
where the time goes in v1:
time: 603 us; the launch traced here: 593 us
  blocking collectives  233 us (39%)
  Pallas kernels  228 us (38%)
  matrix products  55.4 us (9%)
  local copies, waits for them, and re-layouts  47.4 us (8%)
  other arithmetic  21.9 us (4%)
  between operations  7.14 us (1%)
    psum x3, blocking collectives, means(): return lax.psum(jnp.stack([jnp.sum(v) for v in values]), AXES) / states  233 us
    pallas_call x6, Pallas kernels, exchange(): pl.pallas_call(functools.partial(exchange_kernel, ng, nd), out_shape=jax....  228 us
    dot_general x8, matrix products, local(): return jnp.einsum('pt,tsl->psl', mat, v, precision=HI)  24.1 us
    dot_general x4, matrix products, local(): return jnp.einsum('pk,bkl->bpl', mat, u, precision=HI).reshape(v.shape)  13 us

profile of v1, /device:TPU:32, one launch (start us, length us, event | category | flops | bytes accessed | tf_op | source)
XLA Modules:
  0.0 593.1 jit_solution(15556937495534472887)
XLA Ops:
  0.6 2.2 multiply_reduce_fusion.2
  2.8 79.7 %psum.21 = f32[1]{0:T(128)} all-reduce(f32[1]{0:T(128)} %bitcast), channel_id=1, replica_groups=mesh['grp'=16,'dev'=16] {'grp','dev'}, use_global_device_ids=true, to_apply=%region_1.0 | all-reduce | flops 1 | bytes 8 | tf_op jit(solution)/shard_map/psum | solution.py:89
  83.3 0.6 copy.190
  84.0 2.2 fusion.58
  86.3 1.2 convolution_bitcast_fusion.15
  87.4 1.6 copy.30
  89.0 1.2 reshape_squeeze.17
  90.7 2.4 convolution_bitcast_fusion.14
  93.2 1.6 copy.33
  94.8 2.8 fusion.37
  97.6 1.3 copy.72
  98.9 3.0 bitcast_add_fusion.4.x_ref
  101.9 37.0 %exchange.6 = f32[256,8,128]{2,1,0:T(8,128)} custom-call(f32[256,8,128]{2,1,0:T(8,128)} %bitcast_add_fusion.4.x_ref), custom_call_target="tpu_custom_call" | custom-call | tf_op jit(solution)/shard_map/exchange/pallas_call | solution.py:48
  138.9 38.3 %exchange.7 = f32[256,8,128]{2,1,0:T(8,128)} custom-call(f32[256,8,128]{2,1,0:T(8,128)} %bitcast.241), custom_call_target="tpu_custom_call" | custom-call | tf_op jit(solution)/shard_map/exchange/pallas_call | solution.py:48
  177.2 4.0 convolution_bitcast_fusion.13
  181.2 2.7 copy.35
  183.9 3.7 fusion.18
  187.7 2.6 copy.78
  190.3 1.7 bitcast_add_fusion.3
  192.0 2.8 convolution_bitcast_fusion.12
  194.8 1.3 copy.37
  196.1 3.1 convolution_bitcast_fusion.11
  199.2 1.3 copy.39
  200.5 38.6 %exchange.8 = f32[256,8,128]{2,1,0:T(8,128)} custom-call(f32[256,8,128]{2,1,0:T(8,128)} %bitcast.253), custom_call_target="tpu_custom_call" | custom-call | tf_op jit(solution)/shard_map/exchange/pallas_call | solution.py:48
  239.1 1.8 fusion.57
  240.8 1.2 reshape_squeeze.18
  242.1 1.6 copy.81
  243.7 3.7 convolution_bitcast_fusion.10
  247.4 0.6 copy.42
  248.0 3.8 convolution_bitcast_fusion.9
  251.8 1.6 copy.44
  253.4 1.8 reshape_squeeze.19
  255.2 2.7 multiply_reduce_fusion.1
  258.6 1.3 fusion.8
  259.8 1.4 pad_maximum_fusion
  261.2 76.7 %psum.22 = f32[2]{0:T(128)S(1)} all-reduce(f32[2]{0:T(128)S(1)} %pad_maximum_fusion), channel_id=1, replica_groups=mesh['grp'=16,'dev'=16] {'grp','dev'}, use_global_device_ids=true, to_apply=%region_4.0 | all-reduce | flops 2 | bytes 16 | tf_op jit(solution)/shard_map/psum | solution.py:89
  340.4 1.2 fusion.9.x_ref
  341.6 2.1 convolution_bitcast_fusion.6
  344.3 1.2 convolution_bitcast_fusion.7
  345.5 1.6 copy.50
  347.1 2.8 fusion.16
  349.9 1.3 copy.88
  351.2 2.8 bitcast_add_fusion.1.x_ref
  354.0 37.3 %exchange.9 = f32[256,8,128]{2,1,0:T(8,128)} custom-call(f32[256,8,128]{2,1,0:T(8,128)} %bitcast_add_fusion.1.x_ref), custom_call_target="tpu_custom_call" | custom-call | tf_op jit(solution)/shard_map/exchange/pallas_call | solution.py:48
  391.2 38.5 %exchange.10 = f32[256,8,128]{2,1,0:T(8,128)} custom-call(f32[256,8,128]{2,1,0:T(8,128)} %copy-done), custom_call_target="tpu_custom_call" | custom-call | tf_op jit(solution)/shard_map/exchange/pallas_call | solution.py:48
  429.8 3.1 convolution_bitcast_fusion.5
  432.9 1.3 copy.55
  434.2 2.8 fusion.14
  437.0 1.3 copy.94
  438.3 1.7 bitcast_add_fusion
  440.0 2.8 convolution_bitcast_fusion.4
  443.2 2.8 convolution_bitcast_fusion.3
  446.0 1.4 copy.59
  447.3 38.4 %exchange.11 = f32[256,8,128]{2,1,0:T(8,128)} custom-call(f32[256,8,128]{2,1,0:T(8,128)} %bitcast.256), custom_call_target="tpu_custom_call" | custom-call | tf_op jit(solution)/shard_map/exchange/pallas_call | solution.py:48
  485.7 3.3 convolution_bitcast_fusion.2
  489.7 2.8 convolution_bitcast_fusion.1
  493.4 1.8 multiply_reduce_fusion
  496.4 1.3 fusion
  497.7 2.1 pad_maximum_fusion.1
  499.8 76.8 %psum.23 = f32[3]{0:T(128)S(1)} all-reduce(f32[3]{0:T(128)S(1)} %pad_maximum_fusion.1), channel_id=1, replica_groups=mesh['grp'=16,'dev'=16] {'grp','dev'}, use_global_device_ids=true, to_apply=%region_8.0 | all-reduce | flops 3 | bytes 24 | tf_op jit(solution)/shard_map/psum | solution.py:89
  576.6 0.7 fusion.60
  580.6 1.2 pad_maximum_fusion.2
  581.8 2.0 fusion.3
  584.3 8.6 %copy.189 = f32[1,2,2048,128]{3,1,2,0:T(2,128)} copy(f32[1,2,2048,128]{3,2,1,0:T(8,128)S(1)} %bitcast.244) | data formatting | bytes 4194304
  (36 shorter events, 6.2 us)
Async XLA Ops:
  0.6 82.6 %copy-start.7 = (f32[262144]{0:T(1024)S(1)}, f32[262144]{0:T(1024)}, u32[]{:S(2)}) copy-start(f32[262144]{0:T(1024)} %param.3) | copy-start | bytes 3145732
  83.9 3.5 copy-start.4
  181.2 2.7 copy-start.5
  187.7 2.6 copy-start.8
  243.7 3.7 copy-start.2
  341.6 5.5 copy-start
  432.9 1.3 copy-start.6
  437.0 1.3 copy-start.9
  447.3 38.4 %copy-start.3 = (f32[8,32,8,32,1]{1,2,3,0,4:T(8,128)S(1)}, f32[8,32,8,32,1]{1,2,3,0,4:T(8,128)}, u32[]{:S(2)}) copy-start(f32[8,32,8,32,1]{1,2,3,0,4:T(8,128)} %copy-done.2) | copy-start | bytes 786436
  492.4 1.0 copy-start.10
  495.2 1.2 copy-start.1

commit v2 on v1

v2 whole, which is shorter than its diff:
```python
import functools

import jax
import jax.numpy as jnp
from jax import lax
from jax.experimental import pallas as pl
from jax.experimental.pallas import tpu as pltpu
from jax.sharding import PartitionSpec as P

MESH = pl.DeviceIdType.MESH
F32 = jnp.float32
BF16 = jnp.bfloat16
AXES = ("grp", "dev")
EPS = 1e-06


def in_two(value):
    high = value.astype(BF16)
    return high, (value - high.astype(F32)).astype(BF16)


def kernel(
    ng, nd, start_hbm, hopping_hbm, blocks_hbm, basis_ref, hess_ref,
    natural, hopping, blocks, mats, x_ref, part, total, image, second, fetched,
    share, shares, load_sem, send_sem, recv_sem, share_send, share_recv,
):
    n = ng * nd
    states = float(n * n * 8 * 128)
    grp, dev = lax.axis_index("grp"), lax.axis_index("dev")
    me = grp * nd + dev
    quarter = n // 4
    barrier = pltpu.get_barrier_semaphore()

    loads = [
        pltpu.make_async_copy(start_hbm, natural, load_sem.at[0]),
        pltpu.make_async_copy(hopping_hbm, hopping, load_sem.at[1]),
        pltpu.make_async_copy(blocks_hbm, blocks, load_sem.at[2]),
    ]
    for load in loads:
        load.start()

    def greet(off, carry):
        to = lax.rem(me + off, n)
        pl.semaphore_signal(barrier, inc=1, device_id=(to // nd, to % nd), device_id_type=MESH)
        return carry

    lax.fori_loop(1, n, greet, 0)


    def send_some(src, which, first):
        dst = fetched.at[which]

        def send(j, carry):
            to = first + lax.rem(me + j, quarter)

            @pl.when(to != me)
            def _():
                pltpu.make_async_remote_copy(
                    src_ref=src.at[pl.ds(pl.multiple_of(to * 8, 8), 8)],
                    dst_ref=dst.at[pl.ds(pl.multiple_of(me * 8, 8), 8)],
                    send_sem=send_sem.at[which],
                    recv_sem=recv_sem.at[which],
                    device_id=(to // nd, to % nd),
                    device_id_type=MESH,
                ).start()

            return carry

        lax.fori_loop(0, quarter, send, 0)

    def keep_own(src, which):
        own = pl.ds(pl.multiple_of(me * 8, 8), 8)
        fetched[which, own, :] = src[own, :]

    def quarter_of(i):
        return lax.rem(me // quarter + i, 4)

    def send_all(src, which):
        def body(i, carry):
            send_some(src, which, quarter_of(i) * quarter)
            return carry

        lax.fori_loop(0, 4, body, 0)
        keep_own(src, which)

    def wait_fetched(which):
        got = fetched.at[which, pl.ds(0, (n - 1) * 8)]
        pltpu.make_async_copy(got, got, recv_sem.at[which]).wait()

    def wait_sent(which):
        got = fetched.at[which, pl.ds(0, (n - 1) * 8)]
        pltpu.make_async_copy(got, got, send_sem.at[which]).wait()


    def prepare(stack, index, slot):
        high, low = in_two(stack[index])
        mats[slot, :, 0:256] = high
        mats[slot, :, 256:512] = low
        mats[slot, :, 512:768] = high

    def times(slot, x):
        high, low = in_two(x)
        return jnp.dot(
            mats[slot], jnp.concatenate([high, high, low], 0), preferred_element_type=F32
        )

    def rows_of(window, b):
        if window in (1, 4):
            return [pl.ds(b, 256, stride=8)]
        if window == 2:
            return [pl.ds(b * 8 + s, 32, stride=64) for s in range(8)]
        return [pl.ds(pl.multiple_of(b * 256, 256), 256)]

    def column_block(window, slot, src, dst, add, i):
        rows = [rows_of(window, 2 * i), rows_of(window, 2 * i + 1)]
        halves = [jnp.concatenate([src[r, :] for r in rs], 0) for rs in rows]
        y = times(slot, jnp.concatenate(halves, 1))
        for h, rs in enumerate(rows):
            size = 256 // len(rs)
            for k, r in enumerate(rs):
                piece = y[k * size : (k + 1) * size, h * 128 : (h + 1) * 128]
                dst[r, :] = dst[r, :] + piece if add else piece

    def row_block(slot, src, dst, add, i):
        rows = pl.ds(pl.multiple_of(i * 512, 512), 512)
        x = src[rows, :].reshape(32, 2, 8, 128)
        x = jnp.concatenate([x[:, 0].reshape(256, 128), x[:, 1].reshape(256, 128)], 1)
        high, low = in_two(x)
        y = lax.dot_general(
            jnp.concatenate([high, high, low], 1),
            mats[slot],
            (((1,), (1,)), ((), ())),
            preferred_element_type=F32,
        )
        y = jnp.stack([y[:, :128].reshape(32, 8, 128), y[:, 128:].reshape(32, 8, 128)], 1)
        y = y.reshape(512, 128)
        dst[rows, :] = dst[rows, :] + y if add else y

    def block(window, slot, src, dst, add, i):
        if window == 0:
            row_block(slot, src, dst, add, i)
        else:
            column_block(window, slot, src, dst, add, i)

    def product(window, slot, src, dst, add=False):
        def body(i, carry):
            block(window, slot, src, dst, add, i)
            return carry

        lax.fori_loop(0, 4, body, 0)

    def product_and_send(window, slot, src, dst, which):
        def body(i, carry):
            q = quarter_of(i)
            block(window, slot, src, dst, False, q)
            send_some(dst, which, q * quarter)
            return carry

        lax.fori_loop(0, 4, body, 0)
        keep_own(dst, which)


    def share_out(k, stage, tile):
        size, at = (nd, dev) if stage == 0 else (ng, grp)
        share[k, stage] = tile
        shares[k, stage, at] = tile
        for off in range(1, size):
            to = lax.rem(at + off, size)
            pltpu.make_async_remote_copy(
                src_ref=share.at[k, stage],
                dst_ref=shares.at[k, stage, at],
                send_sem=share_send.at[k, stage],
                recv_sem=share_recv.at[k, stage],
                device_id=(grp, to) if stage == 0 else (to, dev),
                device_id_type=MESH,
            ).start()

    def gather_in(k, stage):
        size = nd if stage == 0 else ng
        got = shares.at[k, stage, pl.ds(0, size - 1)]
        pltpu.make_async_copy(got, got, share_recv.at[k, stage]).wait()
        pltpu.make_async_copy(got, got, share_send.at[k, stage]).wait()
        return jnp.sum(shares[k, stage, pl.ds(0, size)], 0)

    def means(k):
        tile = jnp.sum(gather_in(k, 1), 1, keepdims=True) / states
        return [tile[i : i + 1] for i in range(3)]

    def partial_sums(terms, count):
        def body(i, carry):
            rows = pl.ds(pl.multiple_of(i * 256, 256), 256)
            return tuple(
                c + jnp.sum(t.reshape(32, 8, 128), 0)
                for c, t in zip(carry, terms(rows), strict=True)
            )

        sums = lax.fori_loop(0, 8, body, (jnp.zeros((8, 128), F32),) * count)
        sums = [jnp.sum(s, 0, keepdims=True) for s in sums]
        return jnp.concatenate(sums + [jnp.zeros((8 - count, 128), F32)], 0)


    loads[0].wait()
    for s in range(8):
        x_ref[pl.ds(s, 256, stride=8), :] = natural[pl.ds(s * 256, 256), :]
    pl.semaphore_wait(barrier, n - 1)
    send_all(x_ref, 0)
    loads[1].wait()
    for index in range(3):
        prepare(hopping, index, index)
    product(1, 1, x_ref, part)
    product(2, 2, x_ref, part, True)
    product(0, 0, x_ref, part, True)
    send_all(part, 1)
    loads[2].wait()
    for index in range(3, 5):
        prepare(hopping, index, index)
    for index in range(5):
        prepare(blocks, index, 5 + index)
    share_out(0, 0, partial_sums(lambda r: (x_ref[r, :] * x_ref[r, :],), 1))

    def upper(which, after_first, after_second):
        wait_fetched(which)
        after_first()
        product(3, 3, fetched.at[which], total)
        product(4, 4, fetched.at[which], total, True)
        wait_fetched(which + 1)

        def add(i, carry):
            rows = pl.ds(pl.multiple_of(i * 256, 256), 256)
            total[rows, :] = total[rows, :] + fetched[which + 1, rows, :]
            return carry

        lax.fori_loop(0, 8, add, 0)
        product(4, 9, total, total)
        product_and_send(3, 8, total, total, which + 2)
        after_second()

    upper(0, lambda: None, lambda: share_out(0, 1, gather_in(0, 0)))
    wait_fetched(2)
    product(2, 7, fetched.at[2], image)
    product(1, 6, image, image)
    wait_sent(1)
    product_and_send(0, 5, image, image, 3)


    product(1, 1, image, part)
    product(2, 2, image, part, True)
    product(0, 0, image, part, True)
    mean_square = means(0)[0]
    scale = 1.0 / jnp.sqrt(mean_square + EPS)

    def first_terms(r):
        return ((x_ref[r, :] * scale) * (image[r, :] * scale),)

    share_out(1, 0, partial_sums(first_terms, 1))
    send_all(part, 4)
    wait_sent(2)
    known = []

    def take_h00():
        h00 = means(1)[0]
        known.append(h00)

        def second_terms(r):
            first = x_ref[r, :] * scale
            left = image[r, :] * scale - h00 * first
            second[r, :] = left
            return (left * left, first * left)

        share_out(2, 0, partial_sums(second_terms, 2))

    upper(3, lambda: share_out(1, 1, gather_in(1, 0)), take_h00)
    h00 = known[0]
    after = natural
    wait_fetched(5)
    product(2, 7, fetched.at[5], after)
    share_out(2, 1, gather_in(2, 0))
    product(1, 6, after, after)
    product(0, 5, after, after)
    left_square, left_first, _ = means(2)
    r1 = jnp.sqrt(left_square + EPS)
    over_r1 = 1.0 / r1

    def third_terms(r):
        moved = (after[r, :] * scale - h00 * (image[r, :] * scale)) * over_r1
        after[r, :] = moved
        return (x_ref[r, :] * scale * moved, second[r, :] * over_r1 * moved, moved * moved)

    share_out(3, 0, partial_sums(third_terms, 3))
    for s in range(8):
        rows = pl.ds(s, 256, stride=8)
        basis_ref[pl.ds(s * 512, 256, stride=2), :] = second[rows, :] * over_r1
    share_out(3, 1, gather_in(3, 0))
    h01, h11, square = means(3)
    gram00 = mean_square * scale * scale
    gram01 = left_first * over_r1
    gram11 = left_square * over_r1 * over_r1
    square = square - 2.0 * (h01 * h01 + h11 * h11)
    square = square + h01 * h01 * gram00 + 2.0 * h01 * h11 * gram01 + h11 * h11 * gram11
    r2 = jnp.sqrt(jnp.maximum(square, 0.0) + EPS)
    over_r2 = 1.0 / r2
    for s in range(8):
        rows = pl.ds(s, 256, stride=8)
        third = after[rows, :] - h01 * (x_ref[rows, :] * scale) - h11 * (second[rows, :] * over_r1)
        basis_ref[pl.ds(s * 512 + 1, 256, stride=2), :] = third * over_r2
    at = lax.broadcasted_iota(jnp.int32, (8, 128), 1)
    hess = jnp.zeros((8, 128), F32)
    for i, value in enumerate((h00, r1, h01, h11, r2)):
        hess = jnp.where(at == i, value, hess)
    hess_ref[...] = hess
    for which in (0, 3, 4, 5):
        wait_sent(which)


def per_device(start, hopping, blocks):
    ng, nd = lax.axis_size("grp"), lax.axis_size("dev")
    rows = start.shape[0] // 128
    anywhere = pl.BlockSpec(memory_space=pl.ANY)
    vmem = pl.BlockSpec(memory_space=pltpu.VMEM)
    vector = pltpu.VMEM((rows, 128), F32)
    dma = pltpu.SemaphoreType.DMA
    basis, hess = pl.pallas_call(
        functools.partial(kernel, ng, nd),
        out_shape=(
            jax.ShapeDtypeStruct((2 * rows, 128), F32),
            jax.ShapeDtypeStruct((8, 128), F32),
        ),
        in_specs=[anywhere] * 3,
        out_specs=(vmem, vmem),
        scratch_shapes=[
            vector,
            pltpu.VMEM(hopping.shape, F32),
            pltpu.VMEM(blocks.shape, F32),
            pltpu.VMEM((10, 256, 768), BF16),
            vector,
            vector,
            vector,
            vector,
            vector,
            pltpu.VMEM((6, rows, 128), F32),
            pltpu.VMEM((4, 2, 8, 128), F32),
            pltpu.VMEM((4, 2, 16, 8, 128), F32),
            dma((3,)),
            dma((6,)),
            dma((6,)),
            dma((4, 2)),
            dma((4, 2)),
        ],
        name="arnoldi",
        compiler_params=pltpu.CompilerParams(
            collective_id=0, has_side_effects=True, vmem_limit_bytes=56 << 20
        ),
    )(start.reshape(rows, 128), hopping, blocks)
    basis = basis.reshape(rows, 2, 128).transpose(1, 0, 2).reshape(2, -1)
    return basis, hess[0, :5]


def solution(mesh):
    return jax.shard_map(
        per_device,
        mesh=mesh,
        in_specs=(P(AXES), P(), P()),
        out_specs=(P(None, AXES), P()),
        check_vma=False,
    )
```

time: 603 us -> 206 us (0.34); the launches traced: 593 us -> 204 us
  blocking collectives: 233 us -> 0 us
  matrix products: 55.4 us -> 0 us
  local copies, waits for them, and re-layouts: 47.4 us -> 3.79 us
  Pallas kernels: 228 us -> 199 us
  other arithmetic: 21.9 us -> 0 us
  between operations: 7.14 us -> 0.64 us
    psum x3 -> x0, blocking collectives: 233 us -> none  [means(): return lax.psum(jnp.stack([jnp.sum(v) for v in values]), AXES) / states]
    dot_general x20 -> x0, matrix products: 55.4 us -> none  [the longest x8 24.1 us: local(): return jnp.einsum('pt,tsl->psl', mat, v, precision=HI)]
    pallas_call x6 -> x1, Pallas kernels: 228 us -> 199 us  [per_device(): pl.pallas_call(functools.partial(kernel, ng, nd), out_shape=(jax.ShapeDty...]
    transpose x13 -> x0, local copies, waits for them, and re-layouts: 15 us -> none  [the longest x4 6.68 us: local(): return jnp.einsum('pk,bkl->bpl', mat, u, precision=HI).reshape(v.shape)]
    dot_general x8 -> x0, local copies, waits for them, and re-layouts: 10.4 us -> none  [local(): return jnp.einsum('pt,tsl->psl', mat, v, precision=HI)]
    add x4 -> x0, other arithmetic: 9.16 us -> none  [the longest x2 5.77 us: apply(): local(0, hopping[0], v) + local(1, hopping[1], v) + local(2, hopping[2], v)]
    another operation x8 -> x0, local copies, waits for them, and re-layouts: 7.68 us -> none  [the longest x4 4.53 us: local(): m = mat.reshape(8, 32, 8, 32)]
    unnamed x23 -> x1, local copies, waits for them, and re-layouts: 9.74 us -> 2.61 us
where the time goes in v2:
time: 206 us; the launch traced here: 204 us
  Pallas kernels  199 us (97%)
  local copies, waits for them, and re-layouts  3.79 us (2%)
    pallas_call x1, Pallas kernels, per_device(): pl.pallas_call(functools.partial(kernel, ng, nd), out_shape=(jax.ShapeDty...  199 us

profile of v2, /device:TPU:32, one launch (start us, length us, event | category | flops | bytes accessed | tf_op | source)
XLA Modules:
  0.0 203.8 jit_solution(10217631403845010072)
XLA Ops:
  0.6 199.4 %arnoldi.1 = (f32[4096,128]{1,0:T(8,128)}, f32[8,128]{1,0:T(8,128)}) custom-call(f32[2048,128]{1,0:T(8,128)} %bitcast.9, f32[5,256,256]{2,1,0:T(8,128)} %hopping_hbm.1, f32[5,256,256]{2,1,0:T(8,128)} %blocks_hbm.1), custom_call_target="tpu_custom_call" | custom-call | tf_op jit(solution)/shard_map/arnoldi/pallas_call | solution.py:322
  200.0 1.2 slice_bitcast_fusion
  201.2 2.6 %copy.7 = f32[2,262144]{1,0:T(2,128)} copy(f32[2,262144]{1,0:T(2,128)} %bitcast.8) | data formatting | bytes 4194304

commit v3 on v2

--- a/solution.py
+++ b/solution.py
@@ -20,8 +20,8 @@
 
 
 def kernel(
-    ng, nd, start_hbm, hopping_hbm, blocks_hbm, basis_ref, hess_ref,
-    natural, hopping, blocks, mats, x_ref, part, total, image, second, fetched,
+    ng, nd, start_hbm, hopping_hbm, blocks_hbm, basis_hbm, hess_ref,
+    natural, hopping, blocks, mats, both, x_ref, part, total, image, second, fetched,
     share, shares, load_sem, send_sem, recv_sem, share_send, share_recv,
 ):
     n = ng * nd
@@ -111,9 +111,12 @@
             return [pl.ds(b * 8 + s, 32, stride=64) for s in range(8)]
         return [pl.ds(pl.multiple_of(b * 256, 256), 256)]
 
-    def column_block(window, slot, src, dst, add, i):
+    def column_block(window, slot, src, dst, add, i, other=None):
         rows = [rows_of(window, 2 * i), rows_of(window, 2 * i + 1)]
-        halves = [jnp.concatenate([src[r, :] for r in rs], 0) for rs in rows]
+        if other is None:
+            halves = [jnp.concatenate([src[r, :] for r in rs], 0) for rs in rows]
+        else:
+            halves = [jnp.concatenate([src[r, :] + other[r, :] for r in rs], 0) for rs in rows]
         y = times(slot, jnp.concatenate(halves, 1))
         for h, rs in enumerate(rows):
             size = 256 // len(rs)
@@ -136,18 +139,18 @@
         y = y.reshape(512, 128)
         dst[rows, :] = dst[rows, :] + y if add else y
 
-    def block(window, slot, src, dst, add, i):
+    def block(window, slot, src, dst, add, i, other=None):
         if window == 0:
             row_block(slot, src, dst, add, i)
         else:
-            column_block(window, slot, src, dst, add, i)
-
-    def product(window, slot, src, dst, add=False):
-        def body(i, carry):
-            block(window, slot, src, dst, add, i)
-            return carry
-
-        lax.fori_loop(0, 4, body, 0)
+            column_block(window, slot, src, dst, add, i, other)
+
+    def product(window, slot, src, dst, add=False, other=None):
+        def body(i, carry):
+            block(window, slot, src, dst, add, i, other)
+            return carry
+
+        lax.fori_loop(0, 4, body, 0, unroll=4)
 
     def product_and_send(window, slot, src, dst, which):
         def body(i, carry):
@@ -160,10 +163,12 @@
         keep_own(dst, which)
 
 
-    def share_out(k, stage, tile):
-        size, at = (nd, dev) if stage == 0 else (ng, grp)
-        share[k, stage] = tile
-        shares[k, stage, at] = tile
+    z, y_low = dev // 2, dev % 2
+
+    def share_out(k, stage, row):
+        size, at = (32, grp * 2 + y_low) if stage == 0 else (8, z)
+        share[k, stage] = row
+        shares[k, stage, at] = row
         for off in range(1, size):
             to = lax.rem(at + off, size)
             pltpu.make_async_remote_copy(
@@ -171,32 +176,41 @@
                 dst_ref=shares.at[k, stage, at],
                 send_sem=share_send.at[k, stage],
                 recv_sem=share_recv.at[k, stage],
-                device_id=(grp, to) if stage == 0 else (to, dev),
+                device_id=(to // 2, z * 2 + to % 2) if stage == 0 else (grp, to * 2 + y_low),
                 device_id_type=MESH,
             ).start()
 
     def gather_in(k, stage):
-        size = nd if stage == 0 else ng
+        size = 32 if stage == 0 else 8
         got = shares.at[k, stage, pl.ds(0, size - 1)]
         pltpu.make_async_copy(got, got, share_recv.at[k, stage]).wait()
         pltpu.make_async_copy(got, got, share_send.at[k, stage]).wait()
         return jnp.sum(shares[k, stage, pl.ds(0, size)], 0)
 
     def means(k):
-        tile = jnp.sum(gather_in(k, 1), 1, keepdims=True) / states
-        return [tile[i : i + 1] for i in range(3)]
+        row = gather_in(k, 1) / states
+        return [row[:, i : i + 1] for i in range(3)]
+
+    def add_terms(carry, terms):
+        pairs = zip(carry, terms, strict=True)
+        return tuple(c + jnp.sum(t.reshape(-1, 8, 128), 0) for c, t in pairs)
+
+    def as_row(sums):
+        at = lax.broadcasted_iota(jnp.int32, (1, 128), 1)
+        row = jnp.zeros((1, 128), F32)
+        for i, value in enumerate(sums):
+            value = jnp.sum(jnp.sum(value, 0, keepdims=True), 1, keepdims=True)
+            row = jnp.where(at == i, value, row)
+        return row
+
+    def zeros(count):
+        return (jnp.zeros((8, 128), F32),) * count
 
     def partial_sums(terms, count):
         def body(i, carry):
-            rows = pl.ds(pl.multiple_of(i * 256, 256), 256)
-            return tuple(
-                c + jnp.sum(t.reshape(32, 8, 128), 0)
-                for c, t in zip(carry, terms(rows), strict=True)
-            )
-
-        sums = lax.fori_loop(0, 8, body, (jnp.zeros((8, 128), F32),) * count)
-        sums = [jnp.sum(s, 0, keepdims=True) for s in sums]
-        return jnp.concatenate(sums + [jnp.zeros((8 - count, 128), F32)], 0)
+            return add_terms(carry, terms(pl.ds(pl.multiple_of(i * 256, 256), 256)))
+
+        return as_row(lax.fori_loop(0, 8, body, zeros(count)))
 
 
     loads[0].wait()
@@ -218,24 +232,20 @@
         prepare(blocks, index, 5 + index)
     share_out(0, 0, partial_sums(lambda r: (x_ref[r, :] * x_ref[r, :],), 1))
 
-    def upper(which, after_first, after_second):
-        wait_fetched(which)
-        after_first()
-        product(3, 3, fetched.at[which], total)
-        product(4, 4, fetched.at[which], total, True)
-        wait_fetched(which + 1)
-
-        def add(i, carry):
-            rows = pl.ds(pl.multiple_of(i * 256, 256), 256)
-            total[rows, :] = total[rows, :] + fetched[which + 1, rows, :]
-            return carry
-
-        lax.fori_loop(0, 8, add, 0)
-        product(4, 9, total, total)
-        product_and_send(3, 8, total, total, which + 2)
-        after_second()
-
-    upper(0, lambda: None, lambda: share_out(0, 1, gather_in(0, 0)))
+    def send_part(which, start, stop):
+        def body(i, carry):
+            send_some(part, which, quarter_of(i) * quarter)
+            return carry
+
+        lax.fori_loop(start, stop, body, 0)
+
+    wait_fetched(0)
+    product(3, 3, fetched.at[0], total)
+    product(4, 4, fetched.at[0], total, True)
+    wait_fetched(1)
+    product(4, 9, total, total, other=fetched.at[1])
+    product_and_send(3, 8, total, total, 2)
+    share_out(0, 1, gather_in(0, 0))
     wait_fetched(2)
     product(2, 7, fetched.at[2], image)
     product(1, 6, image, image)
@@ -253,43 +263,51 @@
         return ((x_ref[r, :] * scale) * (image[r, :] * scale),)
 
     share_out(1, 0, partial_sums(first_terms, 1))
-    send_all(part, 4)
+    send_part(4, 0, 2)
     wait_sent(2)
-    known = []
-
-    def take_h00():
-        h00 = means(1)[0]
-        known.append(h00)
-
-        def second_terms(r):
-            first = x_ref[r, :] * scale
-            left = image[r, :] * scale - h00 * first
-            second[r, :] = left
-            return (left * left, first * left)
-
-        share_out(2, 0, partial_sums(second_terms, 2))
-
-    upper(3, lambda: share_out(1, 1, gather_in(1, 0)), take_h00)
-    h00 = known[0]
+    wait_fetched(3)
+    share_out(1, 1, gather_in(1, 0))
+    send_part(4, 2, 4)
+    keep_own(part, 4)
+    product(3, 3, fetched.at[3], total)
+    product(4, 4, fetched.at[3], total, True)
+    h00 = means(1)[0]
+
+    def second_terms(r):
+        first = x_ref[r, :] * scale
+        left = image[r, :] * scale - h00 * first
+        second[r, :] = left
+        return (left * left, first * left)
+
+    share_out(2, 0, partial_sums(second_terms, 2))
+    wait_fetched(4)
+    product(4, 9, total, total, other=fetched.at[4])
+    share_out(2, 1, gather_in(2, 0))
+    product_and_send(3, 8, total, total, 5)
+    left_square, left_first, _ = means(2)
+    r1 = jnp.sqrt(left_square + EPS)
+    over_r1 = 1.0 / r1
+    for s in range(8):
+        rows = pl.ds(s, 256, stride=8)
+        value = second[rows, :] * over_r1
+        second[rows, :] = value
+        both[pl.ds(s * 512, 256, stride=2), :] = value
+
     after = natural
     wait_fetched(5)
     product(2, 7, fetched.at[5], after)
-    share_out(2, 1, gather_in(2, 0))
     product(1, 6, after, after)
-    product(0, 5, after, after)
-    left_square, left_first, _ = means(2)
-    r1 = jnp.sqrt(left_square + EPS)
-    over_r1 = 1.0 / r1
-
-    def third_terms(r):
-        moved = (after[r, :] * scale - h00 * (image[r, :] * scale)) * over_r1
-        after[r, :] = moved
-        return (x_ref[r, :] * scale * moved, second[r, :] * over_r1 * moved, moved * moved)
-
-    share_out(3, 0, partial_sums(third_terms, 3))
-    for s in range(8):
-        rows = pl.ds(s, 256, stride=8)
-        basis_ref[pl.ds(s * 512, 256, stride=2), :] = second[rows, :] * over_r1
+
+    def last(i, carry):
+        row_block(5, after, after, False, i)
+        rows = pl.ds(pl.multiple_of(i * 512, 512), 512)
+        moved = (after[rows, :] * scale - h00 * (image[rows, :] * scale)) * over_r1
+        after[rows, :] = moved
+        return add_terms(
+            carry, (x_ref[rows, :] * scale * moved, second[rows, :] * moved, moved * moved)
+        )
+
+    share_out(3, 0, as_row(lax.fori_loop(0, 4, last, zeros(3), unroll=2)))
     share_out(3, 1, gather_in(3, 0))
     h01, h11, square = means(3)
     gram00 = mean_square * scale * scale
@@ -299,48 +317,54 @@
     square = square + h01 * h01 * gram00 + 2.0 * h01 * h11 * gram01 + h11 * h11 * gram11
     r2 = jnp.sqrt(jnp.maximum(square, 0.0) + EPS)
     over_r2 = 1.0 / r2
+    writes = []
     for s in range(8):
         rows = pl.ds(s, 256, stride=8)
-        third = after[rows, :] - h01 * (x_ref[rows, :] * scale) - h11 * (second[rows, :] * over_r1)
-        basis_ref[pl.ds(s * 512 + 1, 256, stride=2), :] = third * over_r2
-    at = lax.broadcasted_iota(jnp.int32, (8, 128), 1)
-    hess = jnp.zeros((8, 128), F32)
+        third = after[rows, :] - h01 * (x_ref[rows, :] * scale) - h11 * second[rows, :]
+        both[pl.ds(s * 512 + 1, 256, stride=2), :] = third * over_r2
+        done = pl.ds(s * 512, 512)
+        writes.append(
+            pltpu.make_async_copy(both.at[done], basis_hbm.at[done], load_sem.at[3 + s])
+        )
+        writes[-1].start()
     for i, value in enumerate((h00, r1, h01, h11, r2)):
-        hess = jnp.where(at == i, value, hess)
-    hess_ref[...] = hess
+        hess_ref[i] = value[0, 0]
     for which in (0, 3, 4, 5):
         wait_sent(which)
+    for write in writes:
+        write.wait()
 
 
 def per_device(start, hopping, blocks):
     ng, nd = lax.axis_size("grp"), lax.axis_size("dev")
     rows = start.shape[0] // 128
     anywhere = pl.BlockSpec(memory_space=pl.ANY)
-    vmem = pl.BlockSpec(memory_space=pltpu.VMEM)
     vector = pltpu.VMEM((rows, 128), F32)
     dma = pltpu.SemaphoreType.DMA
+    operands = (start.reshape(rows, 128), hopping, blocks)
     basis, hess = pl.pallas_call(
         functools.partial(kernel, ng, nd),
         out_shape=(
             jax.ShapeDtypeStruct((2 * rows, 128), F32),
-            jax.ShapeDtypeStruct((8, 128), F32),
+            jax.ShapeDtypeStruct((5,), F32),
         ),
-        in_specs=[anywhere] * 3,
-        out_specs=(vmem, vmem),
+        in_specs=[pl.BlockSpec(memory_space=pltpu.HBM)] * 3,
+        out_specs=(anywhere, pl.BlockSpec(memory_space=pltpu.SMEM)),
         scratch_shapes=[
             vector,
             pltpu.VMEM(hopping.shape, F32),
             pltpu.VMEM(blocks.shape, F32),
             pltpu.VMEM((10, 256, 768), BF16),
+            pltpu.VMEM((2 * rows, 128), F32),
             vector,
             vector,
             vector,
             vector,
             vector,
             pltpu.VMEM((6, rows, 128), F32),
-            pltpu.VMEM((4, 2, 8, 128), F32),
-            pltpu.VMEM((4, 2, 16, 8, 128), F32),
-            dma((3,)),
+            pltpu.VMEM((4, 2, 1, 128), F32),
+            pltpu.VMEM((4, 2, 32, 1, 128), F32),
+            dma((11,)),
             dma((6,)),
             dma((6,)),
             dma((4, 2)),
@@ -348,11 +372,11 @@
         ],
         name="arnoldi",
         compiler_params=pltpu.CompilerParams(
-            collective_id=0, has_side_effects=True, vmem_limit_bytes=56 << 20
+            collective_id=0, has_side_effects=True, vmem_limit_bytes=32 << 20
         ),
-    )(start.reshape(rows, 128), hopping, blocks)
+    )(*[pltpu.with_memory_space_constraint(a, pltpu.HBM) for a in operands])
     basis = basis.reshape(rows, 2, 128).transpose(1, 0, 2).reshape(2, -1)
-    return basis, hess[0, :5]
+    return basis, hess
 
 
 def solution(mesh):

time: 206 us -> 194 us (0.942)
  Pallas kernels: 199 us -> 191 us
    pallas_call x1, Pallas kernels: 199 us -> 191 us  [per_device(): pl.pallas_call(functools.partial(kernel, ng, nd), out_shape=(jax.ShapeDty...]
where the time goes in v3:
time: 194 us; the launch traced here: 193 us
  Pallas kernels  191 us (98%)
    pallas_call x1, Pallas kernels, per_device(): pl.pallas_call(functools.partial(kernel, ng, nd), out_shape=(jax.ShapeDty...  191 us

profile of v3, /device:TPU:32, one launch (start us, length us, event | category | flops | bytes accessed | tf_op | source)
XLA Modules:
  0.0 193.2 jit_solution(18034440746814381057)
XLA Ops:
  0.6 190.7 %arnoldi.1 = (f32[4096,128]{1,0:T(8,128)S(1)}, f32[5]{0:T(128)S(1)}) custom-call(f32[2048,128]{1,0:T(8,128)} %bitcast.7, f32[5,256,256]{2,1,0:T(8,128)} %hopping_hbm.1, f32[5,256,256]{2,1,0:T(8,128)} %blocks_hbm.1), custom_call_target="tpu_custom_call" | custom-call | tf_op jit(solution)/shard_map/arnoldi/pallas_call | solution.py:345
  191.3 1.3 copy.8
  192.7 0.5 copy.9

commit v4 on v3

--- a/solution.py
+++ b/solution.py
@@ -17,6 +17,20 @@
 def in_two(value):
     high = value.astype(BF16)
     return high, (value - high.astype(F32)).astype(BF16)
+
+
+def swapped_halves(tiles):
+    far = pltpu.roll(pltpu.roll(tiles, 64, 2), 4, 1)
+    sub = lax.broadcasted_iota(jnp.int32, tiles.shape, 1) < 4
+    lane = lax.broadcasted_iota(jnp.int32, tiles.shape, 2) < 64
+    return jnp.where(sub == lane, tiles, far)
+
+
+def side_by_side(one, two, upper):
+    lane = lax.broadcasted_iota(jnp.int32, one.shape, one.ndim - 1) < 64
+    if upper:
+        return jnp.where(lane, pltpu.roll(one, 64, one.ndim - 1), two)
+    return jnp.where(lane, one, pltpu.roll(two, 64, one.ndim - 1))
 
 
 def kernel(
@@ -47,19 +61,21 @@
     lax.fori_loop(1, n, greet, 0)
 
 
-    def send_some(src, which, first):
+    def send_some(src, which, first, half=None):
         dst = fetched.at[which]
+        size = 8 if half is None else 4
 
         def send(j, carry):
             to = first + lax.rem(me + j, quarter)
 
             @pl.when(to != me)
             def _():
+                there, here = (t * 8 + (half or 0) * 4 for t in (to, me))
                 pltpu.make_async_remote_copy(
-                    src_ref=src.at[pl.ds(pl.multiple_of(to * 8, 8), 8)],
-                    dst_ref=dst.at[pl.ds(pl.multiple_of(me * 8, 8), 8)],
-                    send_sem=send_sem.at[which],
-                    recv_sem=recv_sem.at[which],
+                    src_ref=src.at[pl.ds(pl.multiple_of(there, size), size)],
+                    dst_ref=dst.at[pl.ds(pl.multiple_of(here, size), size)],
+                    send_sem=send_sem.at[which, half or 0],
+                    recv_sem=recv_sem.at[which, half or 0],
                     device_id=(to // nd, to % nd),
                     device_id_type=MESH,
                 ).start()
@@ -75,21 +91,23 @@
     def quarter_of(i):
         return lax.rem(me // quarter + i, 4)
 
-    def send_all(src, which):
+    def send_all(src, which, half=None):
         def body(i, carry):
-            send_some(src, which, quarter_of(i) * quarter)
+            send_some(src, which, quarter_of(i) * quarter, half)
             return carry
 
         lax.fori_loop(0, 4, body, 0)
-        keep_own(src, which)
-
-    def wait_fetched(which):
-        got = fetched.at[which, pl.ds(0, (n - 1) * 8)]
-        pltpu.make_async_copy(got, got, recv_sem.at[which]).wait()
+
+    def wait_for(sems, which, half=None):
+        got = fetched.at[which, pl.ds(0, (n - 1) * (8 if half is None else 4))]
+        pltpu.make_async_copy(got, got, sems.at[which, half or 0]).wait()
+
+    def wait_fetched(which, half=None):
+        wait_for(recv_sem, which, half)
 
     def wait_sent(which):
-        got = fetched.at[which, pl.ds(0, (n - 1) * 8)]
-        pltpu.make_async_copy(got, got, send_sem.at[which]).wait()
+        for half in (None,) if which in (0, 3) else (0, 1):
+            wait_for(send_sem, which, half)
 
 
     def prepare(stack, index, slot):
@@ -111,9 +129,20 @@
             return [pl.ds(b * 8 + s, 32, stride=64) for s in range(8)]
         return [pl.ds(pl.multiple_of(b * 256, 256), 256)]
 
+    def lower_rows(src, b):
+        pieces = [None] * 8
+        for s in range(4):
+            one = src[pl.ds(b * 8 + s, 32, stride=64), :]
+            two = src[pl.ds(b * 8 + 4 + s, 32, stride=64), :]
+            pieces[s] = side_by_side(one, two, False)
+            pieces[4 + s] = side_by_side(one, two, True)
+        return jnp.concatenate(pieces, 0)
+
     def column_block(window, slot, src, dst, add, i, other=None):
         rows = [rows_of(window, 2 * i), rows_of(window, 2 * i + 1)]
-        if other is None:
+        if other == "halves":
+            halves = [lower_rows(src, 2 * i), lower_rows(src, 2 * i + 1)]
+        elif other is None:
             halves = [jnp.concatenate([src[r, :] for r in rs], 0) for rs in rows]
         else:
             halves = [jnp.concatenate([src[r, :] + other[r, :] for r in rs], 0) for rs in rows]
@@ -124,7 +153,7 @@
                 piece = y[k * size : (k + 1) * size, h * 128 : (h + 1) * 128]
                 dst[r, :] = dst[r, :] + piece if add else piece
 
-    def row_block(slot, src, dst, add, i):
+    def row_block(slot, src, dst, add, i, swap=False):
         rows = pl.ds(pl.multiple_of(i * 512, 512), 512)
         x = src[rows, :].reshape(32, 2, 8, 128)
         x = jnp.concatenate([x[:, 0].reshape(256, 128), x[:, 1].reshape(256, 128)], 1)
@@ -137,20 +166,21 @@
         )
         y = jnp.stack([y[:, :128].reshape(32, 8, 128), y[:, 128:].reshape(32, 8, 128)], 1)
         y = y.reshape(512, 128)
-        dst[rows, :] = dst[rows, :] + y if add else y
+        y = dst[rows, :] + y if add else y
+        dst[rows, :] = swapped_halves(y.reshape(64, 8, 128)).reshape(512, 128) if swap else y
 
     def block(window, slot, src, dst, add, i, other=None):
         if window == 0:
-            row_block(slot, src, dst, add, i)
+            row_block(slot, src, dst, add, i, other == "swap")
         else:
             column_block(window, slot, src, dst, add, i, other)
 
-    def product(window, slot, src, dst, add=False, other=None):
+    def product(window, slot, src, dst, add=False, other=None, start=0, stop=4):
         def body(i, carry):
             block(window, slot, src, dst, add, i, other)
             return carry
 
-        lax.fori_loop(0, 4, body, 0, unroll=4)
+        lax.fori_loop(start, stop, body, 0, unroll=stop - start)
 
     def product_and_send(window, slot, src, dst, which):
         def body(i, carry):
@@ -161,6 +191,39 @@
 
         lax.fori_loop(0, 4, body, 0)
         keep_own(dst, which)
+
+    def swap_total():
+        def body(i, carry):
+            rows = pl.ds(pl.multiple_of(i * 512, 512), 512)
+            tiles = total[rows, :].reshape(64, 8, 128)
+            total[rows, :] = swapped_halves(tiles).reshape(512, 128)
+            return carry
+
+        lax.fori_loop(0, 4, body, 0)
+
+    def half_total(half, i):
+        tiles = total.reshape(n, 8, 128)
+        at = [pl.ds(pl.multiple_of((4 * i + j) * 32, 32), 32) for j in range(4)]
+        held = [swapped_halves(tiles[t]) for t in at]
+        pairs = [side_by_side(held[j], held[j + 1], half == 1).reshape(256, 128) for j in (0, 2)]
+        y = times(8, jnp.concatenate(pairs, 1))
+        for j in range(4):
+            back = y[:, (j // 2) * 128 : (j // 2 + 1) * 128].reshape(32, 8, 128)
+            if j % 2 != half:
+                back = pltpu.roll(back, 64, 2)
+            back = swapped_halves(back)
+            tiles[at[j], half * 4 : half * 4 + 4, :] = back[:, half * 4 : half * 4 + 4, :]
+
+    def half_total_and_send(half, which):
+        def body(h, carry):
+            i = lax.rem(me // (2 * quarter) + h, 2)
+            half_total(half, i)
+            for k in range(2):
+                q = 2 * i + lax.rem(me // quarter + k, 2)
+                send_some(total, which, q * quarter, half)
+            return carry
+
+        lax.fori_loop(0, 2, body, 0)
 
 
     z, y_low = dev // 2, dev % 2
@@ -218,13 +281,16 @@
         x_ref[pl.ds(s, 256, stride=8), :] = natural[pl.ds(s * 256, 256), :]
     pl.semaphore_wait(barrier, n - 1)
     send_all(x_ref, 0)
+    keep_own(x_ref, 0)
     loads[1].wait()
     for index in range(3):
         prepare(hopping, index, index)
     product(1, 1, x_ref, part)
     product(2, 2, x_ref, part, True)
-    product(0, 0, x_ref, part, True)
-    send_all(part, 1)
+    product(0, 0, x_ref, part, True, other="swap")
+    send_all(part, 1, 0)
+    send_all(part, 1, 1)
+    keep_own(part, 1)
     loads[2].wait()
     for index in range(3, 5):
         prepare(hopping, index, index)
@@ -232,22 +298,19 @@
         prepare(blocks, index, 5 + index)
     share_out(0, 0, partial_sums(lambda r: (x_ref[r, :] * x_ref[r, :],), 1))
 
-    def send_part(which, start, stop):
-        def body(i, carry):
-            send_some(part, which, quarter_of(i) * quarter)
-            return carry
-
-        lax.fori_loop(start, stop, body, 0)
-
     wait_fetched(0)
     product(3, 3, fetched.at[0], total)
     product(4, 4, fetched.at[0], total, True)
-    wait_fetched(1)
-    product(4, 9, total, total, other=fetched.at[1])
-    product_and_send(3, 8, total, total, 2)
+    swap_total()
+    for half in range(2):
+        wait_fetched(1, half)
+        product(4, 9, total, total, False, fetched.at[1], 2 * half, 2 * half + 2)
+        half_total_and_send(half, 2)
+    keep_own(total, 2)
     share_out(0, 1, gather_in(0, 0))
-    wait_fetched(2)
-    product(2, 7, fetched.at[2], image)
+    wait_fetched(2, 0)
+    wait_fetched(2, 1)
+    product(2, 7, fetched.at[2], image, other="halves")
     product(1, 6, image, image)
     wait_sent(1)
     product_and_send(0, 5, image, image, 3)
@@ -255,7 +318,7 @@
 
     product(1, 1, image, part)
     product(2, 2, image, part, True)
-    product(0, 0, image, part, True)
+    product(0, 0, image, part, True, other="swap")
     mean_square = means(0)[0]
     scale = 1.0 / jnp.sqrt(mean_square + EPS)
 
@@ -263,14 +326,15 @@
         return ((x_ref[r, :] * scale) * (image[r, :] * scale),)
 
     share_out(1, 0, partial_sums(first_terms, 1))
-    send_part(4, 0, 2)
+    send_all(part, 4, 0)
     wait_sent(2)
     wait_fetched(3)
     share_out(1, 1, gather_in(1, 0))
-    send_part(4, 2, 4)
+    send_all(part, 4, 1)
     keep_own(part, 4)
     product(3, 3, fetched.at[3], total)
     product(4, 4, fetched.at[3], total, True)
+    swap_total()
     h00 = means(1)[0]
 
     def second_terms(r):
@@ -280,10 +344,13 @@
         return (left * left, first * left)
 
     share_out(2, 0, partial_sums(second_terms, 2))
-    wait_fetched(4)
-    product(4, 9, total, total, other=fetched.at[4])
-    share_out(2, 1, gather_in(2, 0))
-    product_and_send(3, 8, total, total, 5)
+    for half in range(2):
+        wait_fetched(4, half)
+        product(4, 9, total, total, False, fetched.at[4], 2 * half, 2 * half + 2)
+        if half == 1:
+            share_out(2, 1, gather_in(2, 0))
+        half_total_and_send(half, 5)
+    keep_own(total, 5)
     left_square, left_first, _ = means(2)
     r1 = jnp.sqrt(left_square + EPS)
     over_r1 = 1.0 / r1
@@ -294,8 +361,9 @@
         both[pl.ds(s * 512, 256, stride=2), :] = value
 
     after = natural
-    wait_fetched(5)
-    product(2, 7, fetched.at[5], after)
+    wait_fetched(5, 0)
+    wait_fetched(5, 1)
+    product(2, 7, fetched.at[5], after, other="halves")
     product(1, 6, after, after)
 
     def last(i, carry):
@@ -365,8 +433,8 @@
             pltpu.VMEM((4, 2, 1, 128), F32),
             pltpu.VMEM((4, 2, 32, 1, 128), F32),
             dma((11,)),
-            dma((6,)),
-            dma((6,)),
+            dma((6, 2)),
+            dma((6, 2)),
             dma((4, 2)),
             dma((4, 2)),
         ],

time: 194 us -> 182 us (0.938)
  Pallas kernels: 191 us -> 178 us
    pallas_call x1, Pallas kernels: 191 us -> 178 us  [per_device(): pl.pallas_call(functools.partial(kernel, ng, nd), out_shape=(jax.ShapeDty...]
where the time goes in v4:
time: 182 us; the launch traced here: 181 us
  Pallas kernels  178 us (98%)
  local copies, waits for them, and re-layouts  1.83 us (1%)
    pallas_call x1, Pallas kernels, per_device(): pl.pallas_call(functools.partial(kernel, ng, nd), out_shape=(jax.ShapeDty...  178 us

profile of v4, /device:TPU:32, one launch (start us, length us, event | category | flops | bytes accessed | tf_op | source)
XLA Modules:
  0.0 180.8 jit_solution(18044021417775244320)
XLA Ops:
  0.6 178.3 %arnoldi.1 = (f32[4096,128]{1,0:T(8,128)S(1)}, f32[5]{0:T(128)S(1)}) custom-call(f32[2048,128]{1,0:T(8,128)} %bitcast.7, f32[5,256,256]{2,1,0:T(8,128)} %hopping_hbm.1, f32[5,256,256]{2,1,0:T(8,128)} %blocks_hbm.1), custom_call_target="tpu_custom_call" | custom-call | tf_op jit(solution)/shard_map/arnoldi/pallas_call | solution.py:413
  178.9 1.3 copy.8
  180.2 0.5 copy.9
